TPU v7x, 128 devices: a whole 4x4x4 slice. The times are simulated.
128 devices in a mesh: row: 16 (over y, z), col: 8 (over x, core).
Axes of the slice: x: 4, y: 4, z: 4, core: 2. Of those that a mesh axis runs over, the one named last changes fastest.
Arguments:
- front: float32 [2, 8192, 4, 4096], P(None, 'row', None, 'col')
- child_blocks: float32 [2, 8192, 8192], P(None, 'row', 'col')
- index_maps: int32 [2, 8192], replicated, may hold values from 0 to 16383, as said below
Outputs:
- schur: float32 [2, 8192, 4, 4096], P(None, 'row', None, 'col')
- factor: float32 [2, 8192, 1024], P(None, 'row')
Inputs may be any that keep to these rules, and one draw needn't show every extreme that they name: Within one child the map names distinct front indices. Entry index_maps[h, (s * R + k) * 32 + i], with R the number of row indices, names an index in a block b of 512 indices with b mod R equal to k.
All inputs are finite; a program needn't handle non-finite values.
Results may differ from a plain program's by a relative error of at most 0.0001.
Values sent between devices are 32-bit elements; how exact they have to be, the bound alone decides.
A program may use at most 128 MiB of HBM per device.

v0:
```python
import jax
import jax.numpy as jnp
from jax import lax
from jax.sharding import PartitionSpec as P

NB = 512


def spread(value, axis, source):
    kept = jnp.where(lax.axis_index(axis) == source, value, 0).astype(value.dtype)
    return lax.psum(kept, axis)


def share_panel(values, root):
    return spread(values, "col", root)


def factor_panel(panel, section, my_row, row_count):
    pivot = spread(panel[:NB], "row", section)
    lower = jnp.linalg.cholesky(pivot)
    solved = lax.linalg.triangular_solve(
        lower, panel, left_side=False, lower=True, transpose_a=True
    )
    rows_local = panel.shape[0]
    block_ids = jnp.arange(rows_local, dtype=jnp.int32) // NB * row_count + my_row
    tiled = jnp.tile(lower, (rows_local // NB, 1))
    zeros = jnp.zeros_like(solved)
    picked = jnp.where((block_ids == section)[:, None], tiled, solved)
    return jnp.where((block_ids < section)[:, None], zeros, picked)


def column_rows(factor_rows, my_col, row_count, col_count):
    pieces = [
        spread(factor_rows, "row", my_col + turn * col_count)
        for turn in range(row_count // col_count)
    ]
    blocks = factor_rows.shape[0] // NB
    shaped = [piece.reshape(blocks, NB, NB) for piece in pieces]
    return jnp.stack(shaped, axis=1).reshape(-1, NB)


def outer_update(matrix, left_rows, right_rows):
    return matrix - jnp.dot(
        left_rows, right_rows.T, precision=lax.Precision.HIGHEST, preferred_element_type=jnp.float32
    )


def group_columns(blocks, row_count, col_count):
    children, height, width = blocks.shape
    ratio = row_count // col_count
    shaped = blocks.reshape(children, height, ratio, ratio, col_count, -1)
    return shaped.transpose(0, 1, 4, 2, 3, 5).reshape(children, height, width)


def local_position(global_ids, count):
    return global_ids // (NB * count) * NB + global_ids % NB


def inverse_map(positions, length):
    arriving = jnp.arange(positions.shape[0], dtype=jnp.int32)
    inverse = jnp.full((length,), -1, jnp.int32).at[positions].set(arriving)
    return (jnp.maximum(inverse, 0), inverse >= 0)


def on_device(front, child_blocks, index_maps):
    row_blocks, block_rows, col_blocks, block_cols = front.shape
    rows_local = row_blocks * block_rows
    cols_local = col_blocks * block_cols
    row_count = lax.axis_size("row")
    col_count = lax.axis_size("col")
    my_row = lax.axis_index("row")
    my_col = lax.axis_index("col")
    summed = front.reshape(rows_local, cols_local)
    outgoing = group_columns(child_blocks, row_count, col_count)
    arrived = lax.all_to_all(
        lax.all_to_all(outgoing, "row", split_axis=1, concat_axis=1, tiled=True),
        "col",
        split_axis=2,
        concat_axis=2,
        tiled=True,
    )
    children = child_blocks.shape[0]
    ratio = row_count // col_count
    row_ids = lax.dynamic_index_in_dim(
        index_maps.reshape(children, row_count, row_count, -1), my_row, 2, keepdims=False
    ).reshape(children, -1)
    col_ids = lax.dynamic_index_in_dim(
        index_maps.reshape(children, col_count, ratio, ratio, col_count, -1),
        my_col,
        4,
        keepdims=False,
    ).reshape(children, -1)
    local_rows = local_position(row_ids, row_count)
    local_cols = local_position(col_ids, col_count)
    for child in range(children):
        row_take, row_valid = inverse_map(local_rows[child], rows_local)
        col_take, col_valid = inverse_map(local_cols[child], cols_local)
        widened = jnp.where(col_valid[None, :], jnp.take(arrived[child], col_take, axis=1), 0.0)
        placed = jnp.where(row_valid[:, None], jnp.take(widened, row_take, axis=0), 0.0)
        summed = summed + placed
    panel = share_panel(summed[:, :NB], 0)
    outputs = []
    for section in range(2):
        factor_rows = factor_panel(panel, section, my_row, row_count)
        factor_cols = column_rows(factor_rows, my_col, row_count, col_count)
        summed = outer_update(summed, factor_rows, factor_cols)
        outputs.append(factor_rows)
        if section == 0:
            panel = share_panel(summed[:, :NB], 1)
    schur = summed.reshape(front.shape)
    factor = jnp.concatenate(outputs, axis=1).reshape(row_blocks, block_rows, 2 * NB)
    return (schur, factor)


def solution(mesh):
    placed = (P(None, "row", None, "col"), P(None, "row", "col"), P())
    return jax.shard_map(
        on_device,
        mesh=mesh,
        in_specs=placed,
        out_specs=(P(None, "row", None, "col"), P(None, "row", None)),
        check_vma=False,
    )
```

profile of v0, /device:TPU:1, one launch (start us, length us, event | category | flops | bytes accessed | tf_op | source)
XLA Modules:
  0.0 1176.0 jit_solution(15224041002027477895)
XLA Ops:
  7.2 5.4 copy.66
  12.5 5.0 copy.67
  17.5 7.3 copy.68
  24.8 57.9 %all_to_all.10 = f32[2,512,1024]{2,0,1:T(2,128)} all-to-all(f32[2,512,1024]{2,0,1:T(2,128)} %copy.68), channel_id=1, replica_groups=mesh['row'=16,'col'=8] {'row'}, dimensions={1} | all-to-all | bytes 8388608 | tf_op jit(solution)/shard_map/all_to_all | solution.py:76
  82.7 9.2 copy.69
  91.9 7.1 all-to-all-start.1
  99.7 10.9 copy.110
  110.6 9.3 copy.102
  119.9 4.3 scatter_custom_fusion.1
  126.8 4.3 scatter_custom_fusion.3
  131.1 2.9 scatter_custom_fusion.2
  134.1 13.8 %all-to-all-done.1 = f32[2,512,1024]{1,0,2:T(2,128)} async-done(((f32[2,512,1024]{1,0,2:T(2,128)}), f32[2,512,1024]{1,0,2:T(2,128)}, u32[]{:S(2)}, u32[]{:S(2)}) %all-to-all-start.1) | async-done | bytes 4194336 | tf_op jit(solution)/shard_map/all_to_all | solution.py:75
  147.9 7.1 fusion.97
  156.7 11.1 gather_fusion
  167.8 3.9 bitcast_select_fusion.1
  171.8 5.4 copy.71
  177.2 11.0 gather_fusion.1
  188.2 9.3 copy.72
  197.5 8.9 gather_fusion.2
  206.4 3.9 bitcast_select_fusion
  210.3 5.4 copy.74
  215.7 11.0 gather_fusion.3
  226.8 9.3 copy.75
  236.0 9.9 fusion
  245.9 3.4 copy-done.1
  250.9 60.6 %all-reduce.10.cloned.1.call-done = f32[1024,512]{0,1:T(8,128)} async-done(((f32[1024,512]{0,1:T(8,128)}), f32[1024,512]{0,1:T(8,128)}) %all-reduce.10.cloned.1.call-update) | async-done | bytes 2097168 | tf_op jit(solution)/shard_map/psum | solution.py:11
  314.1 88.5 %all-reduce.12.cloned.1.call-done = f32[512,512]{0,1:T(8,128)} async-done(((f32[512,512]{0,1:T(8,128)}), f32[512,512]{0,1:T(8,128)}) %all-reduce.12.cloned.1.call-update) | async-done | bytes 1048592 | tf_op jit(solution)/shard_map/psum | solution.py:11
  404.5 11.7 cholesky.286
  416.4 9.8 custom-call.27
  426.9 11.7 cholesky.305
  439.9 10.0 custom-call.28
  450.6 11.7 cholesky.326
  463.0 9.8 custom-call.29
  473.4 11.7 cholesky.343
  490.3 11.9 %while.4 = (s32[]{:T(128)}, f32[512,512]{1,0:T(8,128)}, s32[4,2]{0,1:T(2,128)S(1)}, f32[4,128,128]{2,1,0:T(8,128)S(1)}, s32[]{:T(128)}) while((s32[]{:T(128)}, f32[512,512]{1,0:T(8,128)}, s32[4,2]{0,1:T(2,128)S(1)}, f32[4,128,128]{2,1,0:T(8,128)S(1)}, s32[]{:T(128)}) %tuple.76), condition=%wide.while_cond, body=%wide.while_body.sunk | while | flops 2 | bytes 131181 | solution.py:21
  502.2 39.3 %custom-call.30 = f32[4,128,128]{1,2,0:T(8,128)S(1)} custom-call(f32[4,128,128]{2,1,0:T(8,128)S(1)} %get-tuple-element.20), custom_call_target="InvertDiagBlocksLowerTriangular" | custom-call | tf_op jit(solution)/shard_map/triangular_solve/custom-call.3 | solution.py:21
  558.3 2.9 copy.104
  561.3 2.9 copy.103
  564.4 104.1 %all-reduce.20.cloned.1.call-done = (f32[2,1,512,512]{3,2,1,0:T(8,128)}, f32[2,1,512,512]{3,2,1,0:T(8,128)}) async-done(((f32[2,1,512,512]{3,2,1,0:T(8,128)}, f32[2,1,512,512]{3,2,1,0:T(8,128)}), (f32[2,1,512,512]{3,2,1,0:T(8,128)}, f32[2,1,512,512]{3,2,1,0:T(8,128)})) %all-reduce.20.cloned.1.call-update) | async-done | bytes 4194320 | tf_op jit(solution)/shard_map/psum | solution.py:11
  668.5 2.7 pad_maximum_fusion
  671.2 17.1 %convolution_subtract_fusion.1 = f32[1024,2048]{0,1:T(8,128)S(1)} fusion(f32[1024,2048]{0,1:T(8,128)} %copy-done.1, f32[1024,512]{0,1:T(8,128)S(1)} %get-tuple-element.55, f32[2048,512]{1,0:T(8,128)S(1)} %bitcast.156), kind=kOutput, calls=%fused_computation.22 | convolution fusion | flops 12886999040 | bytes 23068672 | tf_op jit(solution)/shard_map/dot_general | solution.py:43
  688.3 3.4 copy-done
  693.3 63.7 %all-reduce.14.cloned.1.call-done = f32[1024,512]{0,1:T(8,128)} async-done(((f32[1024,512]{0,1:T(8,128)}), f32[1024,512]{0,1:T(8,128)}) %all-reduce.14.cloned.1.call-update) | async-done | bytes 2097168 | tf_op jit(solution)/shard_map/psum | solution.py:11
  759.6 88.4 %all-reduce.16.cloned.1.call-done = f32[512,512]{0,1:T(8,128)} async-done(((f32[512,512]{0,1:T(8,128)}), f32[512,512]{0,1:T(8,128)}) %all-reduce.16.cloned.1.call-update) | async-done | bytes 1048592 | tf_op jit(solution)/shard_map/psum | solution.py:11
  848.0 2.6 copy.84
  853.0 11.7 cholesky.358
  864.9 9.8 custom-call.31
  877.3 11.7 cholesky.377
  890.3 10.2 custom-call.32
  902.1 11.7 cholesky.398
  914.5 9.8 custom-call.33
  925.7 11.7 cholesky.415
  942.4 11.1 while.5
  953.5 39.3 %custom-call.34 = f32[4,128,128]{1,2,0:T(8,128)S(1)} custom-call(f32[4,128,128]{2,1,0:T(8,128)S(1)} %get-tuple-element.21), custom_call_target="InvertDiagBlocksLowerTriangular" | custom-call | tf_op jit(solution)/shard_map/triangular_solve/custom-call.3 | solution.py:21
  1002.9 2.5 copy.85
  1013.3 2.9 copy.106
  1016.2 2.9 copy.105
  1019.2 4.1 pad_maximum_fusion.2
  1023.3 5.3 copy.107
  1028.6 94.9 %all-reduce.18.cloned.1.call-done = (f32[2,1,512,512]{3,2,1,0:T(8,128)}, f32[2,1,512,512]{3,2,1,0:T(8,128)}) async-done(((f32[2,1,512,512]{3,2,1,0:T(8,128)}, f32[2,1,512,512]{3,2,1,0:T(8,128)}), (f32[2,1,512,512]{3,2,1,0:T(8,128)}, f32[2,1,512,512]{3,2,1,0:T(8,128)})) %all-reduce.18.cloned.1.call-update) | async-done | bytes 4194320 | tf_op jit(solution)/shard_map/psum | solution.py:11
  1123.5 2.9 pad_maximum_fusion.1
  1126.4 17.7 %convolution_subtract_fusion = f32[1024,2048]{0,1:T(8,128)} fusion(f32[1024,2048]{0,1:T(8,128)} %copy-done, f32[1024,512]{0,1:T(8,128)S(1)} %copy-done.3, f32[2048,512]{1,0:T(8,128)S(1)} %bitcast.155), kind=kOutput, calls=%fused_computation.21 | convolution fusion | flops 12886999040 | bytes 23068672 | tf_op jit(solution)/shard_map/dot_general | solution.py:43
  1144.1 11.7 reshape.242
  1155.8 13.2 %copy.92 = f32[2,512,4,512]{3,2,1,0:T(4,128)} copy(f32[2,512,4,512]{1,0,3,2:T(2,128)} %reshape.242) | data formatting | bytes 16777216
  (163 shorter events, 92.0 us)
Async XLA Ops:
  91.9 7.1 copy-start.15
  91.9 56.0 %all-to-all-start.1 = ((f32[2,512,1024]{1,0,2:T(2,128)}), f32[2,512,1024]{1,0,2:T(2,128)}, u32[]{:S(2)}, u32[]{:S(2)}) async-start(f32[2,512,1024]{1,0,2:T(2,128)} %copy.69), calls=%async_computation.1 | async-start | bytes 8388608 | tf_op jit(solution)/shard_map/all_to_all | solution.py:75
  99.0 212.5 %all-reduce.10.cloned.1.call-start = ((), (), s32[]{:S(2)}) async-start(), calls=%async_computation.2 | async-start | bytes 4194304 | tf_op jit(solution)/shard_map/psum | solution.py:11
  245.9 3.4 copy-start.1
  250.8 151.8 %all-reduce.12.cloned.1.call-start = ((), (), s32[]{:S(2)}) async-start(), calls=%async_computation.3 | async-start | bytes 2097152 | tf_op jit(solution)/shard_map/psum | solution.py:11
  313.8 354.7 %all-reduce.20.cloned.1.call-start = ((), (), s32[]{:S(2)}) async-start(), calls=%async_computation.7 | async-start | bytes 8388608 | tf_op jit(solution)/shard_map/psum | solution.py:11
  402.6 1.7 copy-start.10
  502.2 43.3 %copy-start.4 = (f32[1024,512]{0,1:T(8,128)S(1)}, f32[1024,512]{0,1:T(8,128)}, u32[]{:S(2)}) copy-start(f32[1024,512]{0,1:T(8,128)} %all-reduce.10.cloned.1.call-done) | copy-start | bytes 6291460
  547.8 2.3 copy-start.8
  553.8 1.0 copy-start.9
  553.8 1.2 copy-start.14
  564.2 192.8 %all-reduce.14.cloned.1.call-start = ((), (), s32[]{:S(2)}) async-start(), calls=%async_computation.4 | async-start | bytes 4194304 | tf_op jit(solution)/shard_map/psum | solution.py:11
  688.3 3.4 copy-start
  693.2 154.7 %all-reduce.16.cloned.1.call-start = ((), (), s32[]{:S(2)}) async-start(), calls=%async_computation.5 | async-start | bytes 2097152 | tf_op jit(solution)/shard_map/psum | solution.py:11
  759.3 364.2 %all-reduce.18.cloned.1.call-start = ((), (), s32[]{:S(2)}) async-start(), calls=%async_computation.6 | async-start | bytes 8388608 | tf_op jit(solution)/shard_map/psum | solution.py:11
  848.0 2.6 copy-start.11
  852.1 1.0 copy-start.12
  992.8 4.2 copy-start.5
  999.2 2.3 copy-start.6
  1007.4 1.0 copy-start.7
  1007.4 1.2 copy-start.13
  1010.5 1.3 copy-start.2
  1123.5 2.9 copy-start.3
Sparse Core Ops, SparseCore 0:
  250.9 60.5 all-reduce.9
  315.3 87.2 all-reduce.11
  564.3 104.1 all-reduce.19
  693.4 63.6 all-reduce.13
  760.7 87.2 all-reduce.15
  1019.3 104.1 all-reduce.17
where the time goes:
time: 1190 us; the launch traced here: 1180 us
  waiting for transfers between devices  514 us (43%)
  other arithmetic  284 us (24%)
  local copies, waits for them, and re-layouts  229 us (19%)
  matrix products  62.1 us (5%)
  blocking collectives  57.9 us (5%)
  between operations  20.1 us (2%)
    psum x6, waiting for transfers between devices, spread(): return lax.psum(kept, axis)  500 us
    another operation x30, other arithmetic, factor_panel(): lower = jnp.linalg.cholesky(pivot)  159 us
    another operation x5, other arithmetic, factor_panel(): lax.linalg.triangular_solve(lower, panel, left_side=False, lower=True, tr...  82.4 us
    all_to_all x1, blocking collectives, on_device(): lax.all_to_all(outgoing, 'row', split_axis=1, concat_axis=1, tiled=True)  57.9 us
    unnamed x38, local copies, waits for them, and re-layouts  46.2 us
    gather x4, local copies, waits for them, and re-layouts, on_device(): jnp.take(widened, row_take, axis=0)  40.6 us
    dot_general x2, matrix products, outer_update(): jnp.dot(left_rows, right_rows.T, precision=lax.Precision.HIGHEST, preferr...  34.9 us
  transfers between devices with their start and end apart: 7, of which 7 were waited for; matrix products, arithmetic and copies ran while one was open for 4% of the time, Pallas kernels for 0%

commit v1 on v0

--- a/solution.py
+++ b/solution.py
@@ -6,9 +6,15 @@
 NB = 512
 
 
+def add_all(x, axis):
+    parts = lax.all_gather(x, axis, axis=0, tiled=False)
+    total = parts.sum(axis=0)
+    return total
+
+
 def spread(value, axis, source):
     kept = jnp.where(lax.axis_index(axis) == source, value, 0).astype(value.dtype)
-    return lax.psum(kept, axis)
+    return add_all(kept, axis)
 
 
 def share_panel(values, root):

time: 1190 us -> 2050 us (1.72)
  waiting for transfers between devices: 514 us -> 1080 us
  local copies, waits for them, and re-layouts: 229 us -> 447 us
  other arithmetic: 284 us -> 352 us
    all_gather x0 -> x8, waiting for transfers between devices: none -> 1070 us  [add_all(): parts = lax.all_gather(x, axis, axis=0, tiled=False)]
    psum x6 -> x0, waiting for transfers between devices: 500 us -> none  [spread(): return lax.psum(kept, axis)]
    unnamed x38 -> x46, local copies, waits for them, and re-layouts: 46.2 us -> 266 us
    reduce_sum x0 -> x8, other arithmetic: none -> 66.4 us  [add_all(): total = parts.sum(axis=0)]
  transfers between devices with their start and end apart: 7 -> 9, of which waited for: 7 -> 9; matrix products, arithmetic and copies ran while one was open for 4% -> 7% of each run, Pallas kernels for 0% -> 0%
where the time goes in v1:
time: 2050 us; the launch traced here: 2040 us
  waiting for transfers between devices  1080 us (53%)
  local copies, waits for them, and re-layouts  447 us (22%)
  other arithmetic  352 us (17%)
  matrix products  69 us (3%)
  blocking collectives  57.9 us (3%)
  between operations  21.2 us (1%)
    all_gather x8, waiting for transfers between devices, add_all(): parts = lax.all_gather(x, axis, axis=0, tiled=False)  1070 us
    unnamed x46, local copies, waits for them, and re-layouts  266 us
    another operation x30, other arithmetic, factor_panel(): lower = jnp.linalg.cholesky(pivot)  159 us
    another operation x5, other arithmetic, factor_panel(): lax.linalg.triangular_solve(lower, panel, left_side=False, lower=True, tr...  83.9 us
    reduce_sum x8, other arithmetic, add_all(): total = parts.sum(axis=0)  66.4 us
    all_to_all x1, blocking collectives, on_device(): lax.all_to_all(outgoing, 'row', split_axis=1, concat_axis=1, tiled=True)  57.9 us
  transfers between devices with their start and end apart: 9, of which 9 were waited for; matrix products, arithmetic and copies ran while one was open for 7% of the time, Pallas kernels for 0%

profile of v1, /device:TPU:1, one launch (start us, length us, event | category | flops | bytes accessed | tf_op | source)
XLA Modules:
  0.0 2038.7 jit_solution(17357912315326132284)
XLA Ops:
  7.2 5.4 copy.62
  17.5 7.3 copy.64
  24.8 57.9 %all_to_all.10 = f32[2,512,1024]{2,0,1:T(2,128)} all-to-all(f32[2,512,1024]{2,0,1:T(2,128)} %copy.64), channel_id=1, replica_groups=mesh['row'=16,'col'=8] {'row'}, dimensions={1} | all-to-all | bytes 8388608 | tf_op jit(solution)/shard_map/all_to_all | solution.py:82
  82.7 9.2 copy.65
  91.9 7.1 all-to-all-start.1
  99.7 10.9 copy.106
  110.6 9.3 copy.92
  133.9 14.1 all-to-all-done.1
  147.9 7.1 fusion.97
  156.7 11.1 gather_fusion.2
  171.8 5.4 copy.70
  177.1 8.9 gather_fusion
  190.0 5.4 copy.67
  195.4 11.0 gather_fusion.1
  206.4 9.3 copy.68
  215.7 11.0 gather_fusion.3
  226.8 9.3 copy.71
  236.0 9.9 fusion
  251.3 81.9 %all-gather.17.cloned.1.call-done = f32[8192,512]{0,1:T(8,128)} async-done(((f32[1024,512]{0,1:T(8,128)}), f32[8192,512]{0,1:T(8,128)}) %all-gather.17.cloned.1.call-update) | async-done | bytes 16777232 | tf_op jit(solution)/shard_map/all_gather | solution.py:10
  333.1 19.7 copy.107
  352.8 5.4 bitcast_reduce_fusion.7
  364.4 106.7 %all-gather.19.cloned.1.call-done = f32[8192,512]{0,1:T(8,128)} async-done(((f32[512,512]{0,1:T(8,128)}), f32[8192,512]{0,1:T(8,128)}) %all-gather.19.cloned.1.call-update) | async-done | bytes 16777232 | tf_op jit(solution)/shard_map/all_gather | solution.py:10
  471.1 20.1 copy.108
  491.3 9.8 bitcast_reduce_fusion.6
  504.8 11.7 cholesky.286
  517.3 9.8 custom-call.27
  529.7 11.9 cholesky.305
  542.3 9.8 custom-call.28
  553.7 11.7 cholesky.326
  566.1 9.8 custom-call.29
  577.8 11.7 cholesky.343
  595.9 11.7 while.4
  608.3 40.3 %custom-call.30 = f32[4,128,128]{1,2,0:T(8,128)S(1)} custom-call(f32[4,128,128]{2,1,0:T(8,128)} %copy-done.12), custom_call_target="InvertDiagBlocksLowerTriangular" | custom-call | tf_op jit(solution)/shard_map/triangular_solve/custom-call.3 | solution.py:27
  664.3 195.3 %all-gather.21.cloned.1.call-done = f32[16384,512]{0,1:T(8,128)} async-done(((f32[1024,512]{0,1:T(8,128)}), f32[16384,512]{0,1:T(8,128)}) %all-gather.21.cloned.1.call-update) | async-done | bytes 33554448 | tf_op jit(solution)/shard_map/all_gather | solution.py:10
  859.6 32.7 %copy.110 = f32[64,8,16,1024]{3,2,1,0:T(8,128)S(1)} copy(f32[64,8,16,1024]{3,1,2,0:T(8,128)} %bitcast.198) | data formatting | bytes 67108864
  892.4 9.7 bitcast_reduce_fusion.3
  905.0 153.6 %all-gather.23.cloned.1.call-done = f32[16384,512]{0,1:T(8,128)} async-done(((f32[1024,512]{0,1:T(8,128)}), f32[16384,512]{0,1:T(8,128)}) %all-gather.23.cloned.1.call-update) | async-done | bytes 33554448 | tf_op jit(solution)/shard_map/all_gather | solution.py:10
  1058.6 32.5 %copy.111 = f32[64,8,16,1024]{3,2,1,0:T(8,128)S(1)} copy(f32[64,8,16,1024]{3,1,2,0:T(8,128)} %bitcast.200) | data formatting | bytes 67108864
  1091.1 9.7 bitcast_reduce_fusion.2
  1106.4 17.5 convolution_subtract_fusion.1
  1128.9 85.0 %all-gather.25.cloned.1.call-done = f32[8192,512]{0,1:T(8,128)} async-done(((f32[1024,512]{0,1:T(8,128)}), f32[8192,512]{0,1:T(8,128)}) %all-gather.25.cloned.1.call-update) | async-done | bytes 16777232 | tf_op jit(solution)/shard_map/all_gather | solution.py:10
  1214.0 19.8 copy.112
  1248.1 105.4 %all-gather.27.cloned.1.call-done = f32[8192,512]{0,1:T(8,128)} async-done(((f32[512,512]{0,1:T(8,128)}), f32[8192,512]{0,1:T(8,128)}) %all-gather.27.cloned.1.call-update) | async-done | bytes 16777232 | tf_op jit(solution)/shard_map/all_gather | solution.py:10
  1353.4 20.2 copy.113
  1373.6 9.8 bitcast_reduce_fusion.4
  1387.2 11.7 cholesky.358
  1399.7 9.8 custom-call.31
  1412.1 12.1 cholesky.377
  1424.9 9.8 custom-call.32
  1436.3 11.7 cholesky.398
  1448.7 9.8 custom-call.33
  1460.1 11.7 cholesky.415
  1478.4 11.7 while.5
  1490.9 40.3 %custom-call.34 = f32[4,128,128]{1,2,0:T(8,128)S(1)} custom-call(f32[4,128,128]{2,1,0:T(8,128)} %copy-done.11), custom_call_target="InvertDiagBlocksLowerTriangular" | custom-call | tf_op jit(solution)/shard_map/triangular_solve/custom-call.3 | solution.py:27
  1552.8 5.6 copy.97
  1558.5 185.5 %all-gather.29.cloned.1.call-done = f32[16384,512]{0,1:T(8,128)} async-done(((f32[1024,512]{0,1:T(8,128)}), f32[16384,512]{0,1:T(8,128)}) %all-gather.29.cloned.1.call-update) | async-done | bytes 33554448 | tf_op jit(solution)/shard_map/all_gather | solution.py:10
  1744.0 32.5 %copy.115 = f32[64,8,16,1024]{3,2,1,0:T(8,128)S(1)} copy(f32[64,8,16,1024]{3,1,2,0:T(8,128)} %bitcast.199) | data formatting | bytes 67108864
  1776.5 8.4 bitcast_reduce_fusion.1
  1786.7 156.3 %all-gather.31.cloned.1.call-done = f32[16384,512]{0,1:T(8,128)} async-done(((f32[1024,512]{0,1:T(8,128)}), f32[16384,512]{0,1:T(8,128)}) %all-gather.31.cloned.1.call-update) | async-done | bytes 33554448 | tf_op jit(solution)/shard_map/all_gather | solution.py:10
  1943.0 32.5 %copy.116 = f32[64,8,16,1024]{3,2,1,0:T(8,128)S(1)} copy(f32[64,8,16,1024]{3,1,2,0:T(8,128)} %bitcast.201) | data formatting | bytes 67108864
  1975.6 8.4 bitcast_reduce_fusion
  1989.0 17.5 convolution_subtract_fusion
  2006.5 11.7 reshape.242
  2018.2 13.2 copy.88
  (187 shorter events, 167.8 us)
Async XLA Ops:
  91.9 7.1 copy-start.10
  91.9 56.0 %all-to-all-start.1 = ((f32[2,512,1024]{1,0,2:T(2,128)}), f32[2,512,1024]{1,0,2:T(2,128)}, u32[]{:S(2)}, u32[]{:S(2)}) async-start(f32[2,512,1024]{1,0,2:T(2,128)} %copy.65), calls=%async_computation.1 | async-start | bytes 8388608 | tf_op jit(solution)/shard_map/all_to_all | solution.py:81
  99.0 234.1 %all-gather.17.cloned.1.call-start = ((), (), s32[]{:S(2)}) async-start(), calls=%async_computation.2 | async-start | bytes 18874368 | tf_op jit(solution)/shard_map/all_gather | solution.py:10
  245.9 3.4 copy-start.1
  250.8 220.3 %all-gather.19.cloned.1.call-start = ((), (), s32[]{:S(2)}) async-start(), calls=%async_computation.3 | async-start | bytes 17825792 | tf_op jit(solution)/shard_map/all_gather | solution.py:10
  359.3 500.4 %all-gather.21.cloned.1.call-start = ((), (), s32[]{:S(2)}) async-start(), calls=%async_computation.4 | async-start | bytes 35651584 | tf_op jit(solution)/shard_map/all_gather | solution.py:10
  503.8 1.0 copy-start.4
  607.6 0.7 copy-start.12
  648.6 3.4 copy-start.7
  648.6 6.7 copy-start.9
  662.7 395.9 %all-gather.23.cloned.1.call-start = ((), (), s32[]{:S(2)}) async-start(), calls=%async_computation.5 | async-start | bytes 35651584 | tf_op jit(solution)/shard_map/all_gather | solution.py:10
  664.3 549.7 %all-gather.25.cloned.1.call-start = ((), (), s32[]{:S(2)}) async-start(), calls=%async_computation.6 | async-start | bytes 18874368 | tf_op jit(solution)/shard_map/all_gather | solution.py:10
  1124.0 3.4 copy-start
  1128.9 224.6 %all-gather.27.cloned.1.call-start = ((), (), s32[]{:S(2)}) async-start(), calls=%async_computation.7 | async-start | bytes 17825792 | tf_op jit(solution)/shard_map/all_gather | solution.py:10
  1239.2 1.3 copy-start.3
  1241.6 502.4 %all-gather.29.cloned.1.call-start = ((), (), s32[]{:S(2)}) async-start(), calls=%async_computation.8 | async-start | bytes 35651584 | tf_op jit(solution)/shard_map/all_gather | solution.py:10
  1386.2 1.0 copy-start.5
  1490.1 0.7 copy-start.11
  1531.2 4.5 copy-start.6
  1531.2 7.9 copy-start.8
  1547.0 396.0 %all-gather.31.cloned.1.call-start = ((), (), s32[]{:S(2)}) async-start(), calls=%async_computation.9 | async-start | bytes 35651584 | tf_op jit(solution)/shard_map/all_gather | solution.py:10
  1986.1 2.9 copy-start.2
Sparse Core Ops, SparseCore 0:
  250.9 82.1 all-gather.16
  359.4 111.6 all-gather.18
  662.8 196.7 all-gather.20
  861.7 196.8 all-gather.22
  1129.0 84.9 all-gather.24
  1241.8 111.6 all-gather.26
  1547.1 196.8 all-gather.28
  1746.2 196.8 all-gather.30
